TPU v7x, 512 devices: a whole 4x8x8 slice. The times are simulated.
512 devices in a mesh: freq: 32 (over z, x_lo, core), tm: 16 (over x_hi, y).
Axes of the slice: x: 4 (x_hi: 2, x_lo: 2; x = x_hi * 2 + x_lo), y: 8, z: 8, core: 2. Of those that a mesh axis runs over, the one named last changes fastest.
Arguments:
- observed: bfloat16 [32, 16, 2, 512, 512], P('freq', 'tm'), may hold values from -6 to 6
- source_beams: bfloat16 [32, 16, 2, 256, 512], P('freq', 'tm'), may hold values from -1.1953125 to 1.1953125
- source_order: int32 [256], replicated, may hold values from 0 to 255, each once
- initial_gains: float32 [32, 2, 32, 512], P('freq'), may hold values from -2 to 2, as said below
- blending: float32 [32, 32], replicated, may hold values from 0 to 1, as said below
Outputs:
- residual: bfloat16 [32, 16, 2, 512, 512], P('freq', 'tm')
- smoothed_gains: float32 [32, 2, 32, 512], P('freq', None, 'tm')
Inputs may be any that keep to these rules, and one draw needn't show every extreme that they name: source_order holds every number of 0 to 255 once. Every row of blending is positive and sums to one. `initial_gains`: every complex gain has a magnitude between 0.5 and 2.
All inputs are finite; a program needn't handle non-finite values.
Results may differ from a plain program's by a relative error of at most 0.0034.
Values sent between devices are 32-bit elements; how exact they have to be, the bound alone decides.
No kernel may reach another device: no remote copies, remote signals or barrier semaphores. Data moves between devices by JAX's collectives and lax.ppermute only.
A program may use at most 64 MiB of HBM per device.

v0:
```python
import jax
import jax.numpy as jnp
from jax import lax
from jax.sharding import PartitionSpec as P

S = 512
K = 32
P_SIZE = 8


def apply_gains(gains, beams):
    real_part = gains[0][:, None, :] * beams[0] - gains[1][:, None, :] * beams[1]
    imag_part = gains[0][:, None, :] * beams[1] + gains[1][:, None, :] * beams[0]
    return jnp.stack([real_part, imag_part]).astype(jnp.bfloat16)


def predict(rounded):
    flat = rounded.reshape(2, rounded.shape[1] * rounded.shape[2], rounded.shape[3])
    joined = flat.reshape(2 * flat.shape[1], flat.shape[2])
    turned = jnp.concatenate([flat[1], -flat[0]], axis=0)
    stacked = jnp.stack([joined, turned])
    return lax.dot_general(
        stacked, joined, (((1,), (0,)), ((), ())), preferred_element_type=jnp.float32
    )


def update(totals, gains):
    denominator = totals[:, 2]
    ratio = jnp.stack([totals[:, 0], totals[:, 1]]) / denominator[None]
    return 0.5 * (ratio + gains)


def local(observed, source_beams, source_order, initial_gains, blending):
    observed_block = observed[0, 0]
    beam_block = source_beams[0, 0]
    start_gains = initial_gains[0]
    highest = lax.Precision.HIGHEST
    beam_float = (
        jnp.take(beam_block, source_order, axis=1).reshape(2, K, P_SIZE, S).astype(jnp.float32)
    )
    seeded = apply_gains(start_gains, beam_float)
    misfit = (observed_block.astype(jnp.float32) - predict(seeded)).astype(jnp.bfloat16)
    seeded_flat = seeded.reshape(2, K * P_SIZE, S)
    owned = K // lax.axis_size("tm")
    stacked = jnp.stack(
        [jnp.stack([seeded_flat[0], -seeded_flat[1]]), jnp.stack([seeded_flat[1], seeded_flat[0]])]
    )
    product = lax.dot_general(
        stacked, misfit, (((1, 3), (0, 2)), ((), ())), preferred_element_type=jnp.float32
    )
    product = product.reshape(2, K, P_SIZE, S)
    pull_real = jnp.sum(beam_float[0] * product[0] + beam_float[1] * product[1], axis=1)
    pull_imag = jnp.sum(beam_float[0] * product[1] - beam_float[1] * product[0], axis=1)
    shaped = seeded_flat.reshape(2, K, P_SIZE, S)
    gram_real = jnp.einsum(
        "kjq,kiq->kji", shaped[0], shaped[0], preferred_element_type=jnp.float32
    ) + jnp.einsum("kjq,kiq->kji", shaped[1], shaped[1], preferred_element_type=jnp.float32)
    gram_imag = jnp.einsum(
        "kjq,kiq->kji", shaped[0], shaped[1], preferred_element_type=jnp.float32
    ) - jnp.einsum("kjq,kiq->kji", shaped[1], shaped[0], preferred_element_type=jnp.float32)
    inner_real = jnp.einsum(
        "kji,kip->kjp", gram_real, beam_float[0], precision=highest
    ) + jnp.einsum("kji,kip->kjp", gram_imag, beam_float[1], precision=highest)
    inner_imag = jnp.einsum(
        "kji,kip->kjp", gram_imag, beam_float[0], precision=highest
    ) - jnp.einsum("kji,kip->kjp", gram_real, beam_float[1], precision=highest)
    denominator = jnp.sum(beam_float[0] * inner_real - beam_float[1] * inner_imag, axis=1)
    pull_real = pull_real + start_gains[0] * denominator
    pull_imag = pull_imag + start_gains[1] * denominator
    local_sums = jnp.stack([pull_real, pull_imag, denominator], axis=1)
    totals = lax.psum(local_sums, "tm")
    damped = update(totals, start_gains)
    mixed = jnp.einsum(
        "fg,gcks->fcks",
        blending,
        lax.all_to_all(damped[None], "freq", split_axis=3, concat_axis=0, tiled=True),
        precision=highest,
    )
    returned = lax.all_to_all(mixed, "freq", split_axis=0, concat_axis=3, tiled=True)
    smooth = returned[0]
    final = apply_gains(smooth, beam_float)
    residual = (observed_block.astype(jnp.float32) - predict(final)).astype(jnp.bfloat16)
    gains_out = lax.dynamic_slice_in_dim(smooth, lax.axis_index("tm") * owned, owned, 1)
    return (residual[None, None], gains_out[None])


def solution(mesh):
    return jax.shard_map(
        local,
        mesh=mesh,
        in_specs=(
            P("freq", "tm", None, None, None),
            P("freq", "tm", None, None, None),
            P(),
            P("freq", None, None, None),
            P(),
        ),
        out_specs=(P("freq", "tm", None, None, None), P("freq", None, "tm", None)),
        check_vma=False,
    )
```

profile of v0, /device:TPU:1, one launch (start us, length us, event | category | flops | bytes accessed | tf_op | source)
XLA Modules:
  0.0 244.0 jit_solution(8187503134172178200)
XLA Ops:
  8.6 1.6 copy.125
  10.4 1.7 gather_fusion
  12.1 1.0 broadcast_select_fusion
  14.0 0.7 fusion.58
  14.7 1.0 slice_bitcast_fusion.3
  16.0 0.7 fusion.60
  17.7 1.8 copy.88
  19.5 1.8 copy.87
  21.2 1.0 copy.89
  22.3 1.9 maximum_bitcast_fusion.2
  24.2 1.1 maximum_bitcast_fusion
  25.3 4.1 %convolution_bitcast_fusion = f32[2,256,512]{2,1,0:T(8,128)} fusion(bf16[1,2,256,512]{3,2,1,0:T(8,128)(2,1)} %get-tuple-element.19, bf16[1,2,256,512]{3,2,1,0:T(8,128)(2,1)} %get-tuple-element.18, bf16[512,512,1]{1,0,2:T(8,128)(2,1)S(1)} %bitcast.168, bf16[1,512,512]{1,2,0:T(8,128)(2,1)} %maximum_bitcast_fusion.2, bf16[1,512,512]{1,2,0:T(8,128)(2,1)} %copy.89, ...), kind=kOutput, calls=%fused_computation.7 | convolution fusion | flops 1076363264 | bytes 4718592 | tf_op jit(solution)/shard_map/dot_general | solution.py:48
  29.4 1.7 fusion.21
  32.7 150.6 %all-reduce.2.cloned.1.call-done = f32[32,3,512]{2,0,1:T(8,128)} async-done(((f32[32,3,512]{2,0,1:T(8,128)}), f32[32,3,512]{2,0,1:T(8,128)}) %all-reduce.2.cloned.1.call-update) | async-done | bytes 196624 | tf_op jit(solution)/shard_map/psum | solution.py:71
  183.3 0.9 slice_bitcast_fusion.6
  185.0 28.3 %all_to_all.33 = f32[32,1,1024]{2,1,0:T(1,128)S(1)} all-to-all(f32[32,1,1024]{2,1,0:T(1,128)S(1)} %reshape.177), channel_id=1, replica_groups=mesh['freq'=32,'tm'=16] {'freq'}, dimensions={0} | all-to-all | bytes 262144 | tf_op jit(solution)/shard_map/all_to_all | solution.py:76
  213.8 0.9 reduce
  216.6 0.9 reshape.179
  217.5 4.0 %all-to-all-start.1 = ((f32[32,1,1024]{2,1,0:T(1,128)}), f32[32,1,1024]{2,1,0:T(1,128)S(1)}, u32[]{:S(2)}, u32[]{:S(2)}) async-start(f32[32,1,1024]{2,1,0:T(1,128)} %reshape.179), calls=%async_computation.1 | async-start | bytes 262144 | tf_op jit(solution)/shard_map/all_to_all | solution.py:79
  221.5 9.4 %all-to-all-done.1 = f32[32,1,1024]{2,1,0:T(1,128)S(1)} async-done(((f32[32,1,1024]{2,1,0:T(1,128)}), f32[32,1,1024]{2,1,0:T(1,128)S(1)}, u32[]{:S(2)}, u32[]{:S(2)}) %all-to-all-start.1) | async-done | bytes 131104 | tf_op jit(solution)/shard_map/all_to_all | solution.py:79
  230.9 1.0 reduce.1
  233.4 0.8 copy.100
  234.3 1.2 copy-done.5
  235.4 1.7 fusion.2
  (53 shorter events, 9.7 us)
Async XLA Ops:
  7.2 208.4 %copy-start = (f32[32,32]{1,0:T(8,128)S(1)}, f32[32,32]{1,0:T(8,128)}, u32[]{:S(2)}) copy-start(f32[32,32]{1,0:T(8,128)} %param.9) | copy-start | bytes 12292
  7.2 3.1 %copy-start.1 = (f32[1,2,32,512]{3,2,1,0:T(8,128)S(1)}, f32[1,2,32,512]{3,2,1,0:T(8,128)}, u32[]{:S(2)}) copy-start(f32[1,2,32,512]{3,2,1,0:T(8,128)} %param.8) | copy-start | bytes 393220
  7.2 176.1 %all-reduce.2.cloned.1.call-start = ((), (), s32[]{:S(2)}) async-start(), calls=%async_computation.2 | async-start | bytes 393216 | tf_op jit(solution)/shard_map/psum | solution.py:71
  22.3 1.9 copy-start.2
  22.3 1.9 copy-start.3
  22.3 1.9 copy-start.4
  217.5 13.4 %all-to-all-start.1 = ((f32[32,1,1024]{2,1,0:T(1,128)}), f32[32,1,1024]{2,1,0:T(1,128)S(1)}, u32[]{:S(2)}, u32[]{:S(2)}) async-start(f32[32,1,1024]{2,1,0:T(1,128)} %reshape.179), calls=%async_computation.1 | async-start | bytes 262144 | tf_op jit(solution)/shard_map/all_to_all | solution.py:79
  234.2 1.2 copy-start.5
Sparse Core Ops, SparseCore 0:
  32.8 150.4 all-reduce.1
where the time goes:
time: 244 us
  waiting for transfers between devices  160 us (66%)
  blocking collectives  28.3 us (12%)
  local copies, waits for them, and re-layouts  16.3 us (7%)
  between operations  14.3 us (6%)
  other arithmetic  12.3 us (5%)
  matrix products  8.76 us (4%)
  starting transfers between devices  4 us (2%)
    psum x1, waiting for transfers between devices, local(): totals = lax.psum(local_sums, 'tm')  151 us
    all_to_all x1, blocking collectives, local(): lax.all_to_all(damped[None], 'freq', split_axis=3, concat_axis=0, tiled=T...  28.3 us
    all_to_all x1, waiting for transfers between devices, local(): lax.all_to_all(mixed, 'freq', split_axis=0, concat_axis=3, tiled=True)  9.43 us
  transfers between devices with their start and end apart: 2, of which 2 were waited for; matrix products, arithmetic and copies ran while one was open for 0% of the time, Pallas kernels for 0%

commit v1 on v0

--- a/solution.py
+++ b/solution.py
@@ -6,6 +6,13 @@
 S = 512
 K = 32
 P_SIZE = 8
+
+
+def trade_parts(array, mesh_axis, split, join):
+    size = lax.axis_size(mesh_axis)
+    blocks = jnp.stack(jnp.split(array, size, axis=split), axis=0)
+    blocks = lax.all_to_all(blocks, mesh_axis, split_axis=0, concat_axis=0)
+    return jnp.concatenate(blocks, axis=join)
 
 
 def apply_gains(gains, beams):
@@ -71,10 +78,7 @@
     totals = lax.psum(local_sums, "tm")
     damped = update(totals, start_gains)
     mixed = jnp.einsum(
-        "fg,gcks->fcks",
-        blending,
-        lax.all_to_all(damped[None], "freq", split_axis=3, concat_axis=0, tiled=True),
-        precision=highest,
+        "fg,gcks->fcks", blending, trade_parts(damped[None], "freq", 3, 0), precision=highest
     )
     returned = lax.all_to_all(mixed, "freq", split_axis=0, concat_axis=3, tiled=True)
     smooth = returned[0]

time: 244 us -> 241 us (0.988)
  other arithmetic: 12.3 us -> 7.53 us
where the time goes in v1:
time: 241 us; the launch traced here: 240 us
  waiting for transfers between devices  160 us (66%)
  blocking collectives  28.3 us (12%)
  local copies, waits for them, and re-layouts  15.3 us (6%)
  between operations  14.7 us (6%)
  matrix products  10.3 us (4%)
  other arithmetic  7.53 us (3%)
  starting transfers between devices  4.18 us (2%)
    psum x1, waiting for transfers between devices, local(): totals = lax.psum(local_sums, 'tm')  150 us
    all_to_all x1, blocking collectives, trade_parts(): blocks = lax.all_to_all(blocks, mesh_axis, split_axis=0, concat_axis=0)  28.3 us
    all_to_all x1, waiting for transfers between devices, local(): lax.all_to_all(mixed, 'freq', split_axis=0, concat_axis=3, tiled=True)  9.43 us
  transfers between devices with their start and end apart: 2, of which 2 were waited for; matrix products, arithmetic and copies ran while one was open for 0% of the time, Pallas kernels for 0%

profile of v1, /device:TPU:1, one launch (start us, length us, event | category | flops | bytes accessed | tf_op | source)
XLA Modules:
  0.0 240.2 jit_solution(7628949097487826763)
XLA Ops:
  7.2 0.7 compare_select_fusion
  8.0 0.7 compare_and_fusion
  8.6 1.6 copy.1651
  10.3 0.7 fusion.62
  11.0 1.7 gather_fusion
  13.3 0.9 fusion.41
  14.2 1.0 broadcast_select_fusion
  15.2 0.9 fusion.36
  16.1 1.0 copy.1602
  17.1 1.0 copy.1603
  18.1 1.1 maximum_bitcast_fusion
  19.2 3.1 %convolution_bitcast_fusion = f32[2,256,512]{2,1,0:T(8,128)S(1)} fusion(bf16[1,2,256,512]{3,2,1,0:T(8,128)(2,1)} %get-tuple-element.21, bf16[1,2,256,512]{3,2,1,0:T(8,128)(2,1)} %get-tuple-element.20, bf16[512,512,1]{1,0,2:T(8,128)(2,1)S(1)} %bitcast.286, bf16[1,512,512]{1,2,0:T(8,128)(2,1)} %bitcast.304, bf16[1,512,512]{1,2,0:T(8,128)(2,1)} %copy.1603, ...), kind=kOutput, calls=%fused_computation.7 | convolution fusion | flops 1076363264 | bytes 4718592 | tf_op jit(solution)/shard_map/dot_general | solution.py:55
  23.4 0.7 fusion.60
  27.2 0.7 pad_maximum_fusion.2
  28.1 150.4 %all-reduce.2.cloned.1.call-done = f32[32,3,512]{2,0,1:T(8,128)} async-done(((f32[32,3,512]{2,0,1:T(8,128)}), f32[32,3,512]{2,0,1:T(8,128)}) %all-reduce.2.cloned.1.call-update) | async-done | bytes 196624 | tf_op jit(solution)/shard_map/psum | solution.py:78
  178.5 0.9 fusion.61
  180.6 28.3 %all_to_all.20 = f32[32,1,1024]{2,1,0:T(1,128)S(1)} all-to-all(f32[32,1,1024]{2,1,0:T(1,128)S(1)} %reshape.181), channel_id=1, replica_groups=mesh['freq'=32,'tm'=16] {'freq'}, dimensions={0} | all-to-all | bytes 262144 | tf_op jit(solution)/shard_map/all_to_all | solution.py:14
  209.3 0.9 reduce
  211.8 0.9 reshape.183
  212.8 4.1 %all-to-all-start.1 = ((f32[32,1,1024]{2,1,0:T(1,128)}), f32[32,1,1024]{2,1,0:T(1,128)S(1)}, u32[]{:S(2)}, u32[]{:S(2)}) async-start(f32[32,1,1024]{2,1,0:T(1,128)} %reshape.183), calls=%async_computation.1 | async-start | bytes 262144 | tf_op jit(solution)/shard_map/all_to_all | solution.py:83
  216.9 9.4 %all-to-all-done.1 = f32[32,1,1024]{2,1,0:T(1,128)S(1)} async-done(((f32[32,1,1024]{2,1,0:T(1,128)}), f32[32,1,1024]{2,1,0:T(1,128)S(1)}, u32[]{:S(2)}, u32[]{:S(2)}) %all-to-all-start.1) | async-done | bytes 131104 | tf_op jit(solution)/shard_map/all_to_all | solution.py:83
  226.3 1.0 reduce.1
  229.7 0.8 copy.1626
  230.4 2.9 %fusion.2 = bf16[1,1,2,512,512]{4,3,2,1,0:T(8,128)(2,1)} fusion(bf16[512,512,1]{1,0,2:T(8,128)(2,1)S(1)} %bitcast.289, bf16[1,512,512]{1,2,0:T(8,128)(2,1)S(1)} %bitcast.305, bf16[1,512,512]{1,2,0:T(8,128)(2,1)S(1)} %copy.1624, bf16[1,1,2,512,512]{4,3,2,1,0:T(8,128)(2,1)} %param.5), kind=kOutput, calls=%fused_computation.5 | convolution fusion | flops 538968064 | bytes 3670016 | tf_op jit(solution)/shard_map/dot_general | solution.py:29
  (100 shorter events, 10.0 us)
Async XLA Ops:
  7.2 203.6 %copy-start = (f32[32,32]{1,0:T(8,128)S(1)}, f32[32,32]{1,0:T(8,128)}, u32[]{:S(2)}) copy-start(f32[32,32]{1,0:T(8,128)} %param.9) | copy-start | bytes 12292
  7.2 3.2 %copy-start.1 = (f32[1,2,32,512]{3,2,1,0:T(8,128)S(1)}, f32[1,2,32,512]{3,2,1,0:T(8,128)}, u32[]{:S(2)}) copy-start(f32[1,2,32,512]{3,2,1,0:T(8,128)} %param.8) | copy-start | bytes 393220
  7.2 171.3 %all-reduce.2.cloned.1.call-start = ((), (), s32[]{:S(2)}) async-start(), calls=%async_computation.2 | async-start | bytes 393216 | tf_op jit(solution)/shard_map/psum | solution.py:78
  8.6 1.6 copy-start.6
  13.2 1.0 copy-start.7
  22.3 0.9 copy-start.5
  23.4 0.9 copy-start.4
  25.7 0.8 copy-start.3
  25.7 1.0 copy-start.2
  212.8 13.6 %all-to-all-start.1 = ((f32[32,1,1024]{2,1,0:T(1,128)}), f32[32,1,1024]{2,1,0:T(1,128)S(1)}, u32[]{:S(2)}, u32[]{:S(2)}) async-start(f32[32,1,1024]{2,1,0:T(1,128)} %reshape.183), calls=%async_computation.1 | async-start | bytes 262144 | tf_op jit(solution)/shard_map/all_to_all | solution.py:83
Sparse Core Ops, SparseCore 0:
  28.0 150.4 all-reduce.1

commit v2 on v0

--- a/solution.py
+++ b/solution.py
@@ -6,6 +6,11 @@
 S = 512
 K = 32
 P_SIZE = 8
+
+
+def gather_and_add(array, axis):
+    shards = lax.all_gather(array, axis)
+    return jnp.sum(shards, axis=0)
 
 
 def apply_gains(gains, beams):
@@ -68,7 +73,7 @@
     pull_real = pull_real + start_gains[0] * denominator
     pull_imag = pull_imag + start_gains[1] * denominator
     local_sums = jnp.stack([pull_real, pull_imag, denominator], axis=1)
-    totals = lax.psum(local_sums, "tm")
+    totals = gather_and_add(local_sums, "tm")
     damped = update(totals, start_gains)
     mixed = jnp.einsum(
         "fg,gcks->fcks",

time: 244 us -> 190 us (0.78)
  waiting for transfers between devices: 160 us -> 109 us
  blocking collectives: 28.3 us -> 20.8 us
  other arithmetic: 12.3 us -> 15.6 us
    psum x1 -> x0, waiting for transfers between devices: 151 us -> none  [local(): totals = lax.psum(local_sums, 'tm')]
    all_gather x0 -> x1, waiting for transfers between devices: none -> 99.8 us  [gather_and_add(): shards = lax.all_gather(array, axis)]
    all_to_all x1, blocking collectives: 28.3 us -> 20.8 us  [local(): lax.all_to_all(damped[None], 'freq', split_axis=3, concat_axis=0, tiled=T...]
where the time goes in v2:
time: 190 us; the launch traced here: 189 us
  waiting for transfers between devices  109 us (57%)
  blocking collectives  20.8 us (11%)
  other arithmetic  15.6 us (8%)
  local copies, waits for them, and re-layouts  15.1 us (8%)
  between operations  14.3 us (8%)
  matrix products  10 us (5%)
  starting transfers between devices  4.18 us (2%)
    all_gather x1, waiting for transfers between devices, gather_and_add(): shards = lax.all_gather(array, axis)  99.8 us
    all_to_all x1, blocking collectives, local(): lax.all_to_all(damped[None], 'freq', split_axis=3, concat_axis=0, tiled=T...  20.8 us
    all_to_all x1, waiting for transfers between devices, local(): lax.all_to_all(mixed, 'freq', split_axis=0, concat_axis=3, tiled=True)  9.43 us
    all_to_all x1, starting transfers between devices, local(): lax.all_to_all(mixed, 'freq', split_axis=0, concat_axis=3, tiled=True)  4.14 us
    dot_general x1, matrix products, local(): lax.dot_general(stacked, misfit, (((1, 3), (0, 2)), ((), ())), preferred_...  4.08 us
  transfers between devices with their start and end apart: 2, of which 2 were waited for; matrix products, arithmetic and copies ran while one was open for 0% of the time, Pallas kernels for 0%

profile of v2, /device:TPU:1, one launch (start us, length us, event | category | flops | bytes accessed | tf_op | source)
XLA Modules:
  0.0 189.2 jit_solution(3832061681936220256)
XLA Ops:
  8.6 1.6 copy.113
  10.3 0.9 slice_bitcast_fusion.10
  11.2 1.7 gather_fusion
  12.9 1.0 broadcast_select_fusion
  14.8 0.7 fusion.58
  15.6 1.0 slice_bitcast_fusion.3
  16.8 0.7 fusion.60
  18.5 1.8 copy.76
  20.3 1.8 copy.75
  22.1 1.0 copy.77
  23.1 1.8 maximum_bitcast_fusion.2
  25.0 2.3 %maximum_bitcast_fusion = (bf16[1,2,256,512]{3,2,1,0:T(8,128)(2,1)}, bf16[1,2,256,512]{3,2,1,0:T(8,128)(2,1)}) fusion(bf16[1,256,512]{2,1,0:T(8,128)(2,1)} %fusion.58, bf16[1,256,512]{2,1,0:T(8,128)(2,1)} %get-tuple-element.15, bf16[1,256,512]{2,1,0:T(8,128)(2,1)} %get-tuple-element.14), kind=kLoop, calls=%fused_computation.31 | loop fusion | flops 524288 | bytes 1835008 | tf_op jit(solution)/shard_map/stack | solution.py:50
  27.3 4.1 %convolution_bitcast_fusion = f32[2,256,512]{2,1,0:T(8,128)} fusion(bf16[1,2,256,512]{3,2,1,0:T(8,128)(2,1)} %get-tuple-element.19, bf16[1,2,256,512]{3,2,1,0:T(8,128)(2,1)} %get-tuple-element.18, bf16[512,512,1]{1,0,2:T(8,128)(2,1)S(1)} %bitcast.169, bf16[1,512,512]{1,2,0:T(8,128)(2,1)} %maximum_bitcast_fusion.2, bf16[1,512,512]{1,2,0:T(8,128)(2,1)} %copy.77, ...), kind=kOutput, calls=%fused_computation.7 | convolution fusion | flops 1076363264 | bytes 4718592 | tf_op jit(solution)/shard_map/dot_general | solution.py:53
  31.4 1.7 fusion.21
  34.7 99.8 %all-gather.3.cloned.1.call-done = f32[512,3,512]{2,0,1:T(8,128)} async-done(((f32[32,3,512]{2,0,1:T(8,128)}), f32[512,3,512]{2,0,1:T(8,128)}) %all-gather.3.cloned.1.call-update) | async-done | bytes 3145744 | tf_op jit(solution)/shard_map/all_gather | solution.py:12
  134.5 2.2 %reduce_sum.48 = f32[32,3,512]{2,0,1:T(8,128)S(1)} reduce(f32[16,32,3,512]{3,1,0,2:T(8,128)} %bitcast.173, f32[]{:T(128)} %constant.7.clone.1), dimensions={0}, to_apply=%region_3.4 | reduce | flops 737280 | bytes 3342340 | tf_op jit(solution)/shard_map/reduce_sum | solution.py:13
  137.5 20.8 %all_to_all.33 = f32[32,1,1024]{2,1,0:T(1,128)S(1)} all-to-all(f32[32,1,1024]{2,1,0:T(1,128)S(1)} %reshape.178), channel_id=1, replica_groups=mesh['freq'=32,'tm'=16] {'freq'}, dimensions={0} | all-to-all | bytes 262144 | tf_op jit(solution)/shard_map/all_to_all | solution.py:81
  158.9 0.9 reduce
  161.6 0.9 reshape.180
  162.6 4.1 %all-to-all-start.1 = ((f32[32,1,1024]{2,1,0:T(1,128)}), f32[32,1,1024]{2,1,0:T(1,128)S(1)}, u32[]{:S(2)}, u32[]{:S(2)}) async-start(f32[32,1,1024]{2,1,0:T(1,128)} %reshape.180), calls=%async_computation.1 | async-start | bytes 262144 | tf_op jit(solution)/shard_map/all_to_all | solution.py:84
  166.7 9.4 %all-to-all-done.1 = f32[32,1,1024]{2,1,0:T(1,128)S(1)} async-done(((f32[32,1,1024]{2,1,0:T(1,128)}), f32[32,1,1024]{2,1,0:T(1,128)S(1)}, u32[]{:S(2)}, u32[]{:S(2)}) %all-to-all-start.1) | async-done | bytes 131104 | tf_op jit(solution)/shard_map/all_to_all | solution.py:84
  176.1 1.0 reduce.1
  178.6 0.8 copy.88
  179.5 2.9 %fusion.2 = bf16[1,1,2,512,512]{4,3,2,1,0:T(8,128)(2,1)} fusion(bf16[512,512,1]{1,0,2:T(8,128)(2,1)S(1)} %bitcast.172, bf16[1,512,512]{1,2,0:T(8,128)(2,1)S(1)} %maximum_bitcast_fusion.3, bf16[1,512,512]{1,2,0:T(8,128)(2,1)S(1)} %copy.86, bf16[1,1,2,512,512]{4,3,2,1,0:T(8,128)(2,1)} %param.5), kind=kOutput, calls=%fused_computation.5 | convolution fusion | flops 538968064 | bytes 3670016 | tf_op jit(solution)/shard_map/dot_general | solution.py:27
  (46 shorter events, 9.7 us)
Async XLA Ops:
  7.2 153.4 %copy-start = (f32[32,32]{1,0:T(8,128)S(1)}, f32[32,32]{1,0:T(8,128)}, u32[]{:S(2)}) copy-start(f32[32,32]{1,0:T(8,128)} %param.9) | copy-start | bytes 12292
  7.2 127.3 %all-gather.3.cloned.1.call-start = ((), (), s32[]{:S(2)}) async-start(), calls=%async_computation.2 | async-start | bytes 3342336 | tf_op jit(solution)/shard_map/all_gather | solution.py:12
  33.0 0.9 copy-start.1
  162.6 13.6 %all-to-all-start.1 = ((f32[32,1,1024]{2,1,0:T(1,128)}), f32[32,1,1024]{2,1,0:T(1,128)S(1)}, u32[]{:S(2)}, u32[]{:S(2)}) async-start(f32[32,1,1024]{2,1,0:T(1,128)} %reshape.180), calls=%async_computation.1 | async-start | bytes 262144 | tf_op jit(solution)/shard_map/all_to_all | solution.py:84
Sparse Core Ops, SparseCore 0:
  34.8 99.6 all-gather.2
